TPU v7x, 32 devices: a whole 2x2x4 slice. The times are simulated.
32 devices in a mesh: prompt: 4 (over x, core), sample: 8 (over z, y).
Axes of the slice: x: 2, y: 2, z: 4, core: 2. Of those that a mesh axis runs over, the one named last changes fastest.
Arguments:
- latent: bfloat16 [1024, 576], P('prompt'), may hold values from -16 to 16
- queries: bfloat16 [1024, 128, 576], P('prompt', 'sample'), may hold values from -64 to 64
- cotangent: bfloat16 [1024, 128, 512], P('prompt', 'sample'), may hold values from -18 to 18
- suffix_out: bfloat16 [1024, 128, 512], P('prompt', 'sample'), may hold values from -6 to 6
- suffix_lse: bfloat16 [1024, 128], P('prompt', 'sample'), may hold values from 6 to 10
- rewards: float32 [4], replicated, may hold values from -5 to 5
- slot_sample: int32 [1024], P('prompt'), may hold values from 0 to 4, as said below
Outputs:
- query_grad: bfloat16 [1024, 128, 576], P('prompt', 'sample')
- latent_grad: float32 [1024, 576], P('prompt')
Inputs may be any that keep to these rules, and one draw needn't show every extreme that they name: `slot_sample`: on every device the live slots come first and the others hold 4. Read over the devices in order, the live slots' completion numbers never fall, and every completion has a slot. Exactly 512 slots are live in all, and some device has all 256 of its slots live.
All inputs are finite; a program needn't handle non-finite values.
Results may differ from a plain program's by a relative error of at most 0.006.
Values may be sent and summed in bfloat16 or wider, within the bound.
A program may use at most 128 MiB of HBM per device.

v0:
```python
import math
import jax
import jax.numpy as jnp
from jax import lax
from jax.sharding import PartitionSpec as P

ROPE = 64
NOPE = 128


def softmax_scale():
    return (0.1 * math.log(40.0) + 1.0) ** 2 / math.sqrt(NOPE + ROPE)


def attend(queries, scaled, suffix_out, suffix_lse, prefix_keys, factor):
    value_width = scaled.shape[-1]
    scores = factor * jnp.einsum(
        "thd,pd->thp", queries, prefix_keys, preferred_element_type=jnp.float32
    )
    row_max = jnp.max(scores, axis=2)
    prefix_lse = row_max + jnp.log(jnp.sum(jnp.exp(scores - row_max[..., None]), axis=2))
    tail_lse = suffix_lse.astype(jnp.float32)
    joint_max = jnp.maximum(prefix_lse, tail_lse)
    total_lse = joint_max + jnp.log(jnp.exp(prefix_lse - joint_max) + jnp.exp(tail_lse - joint_max))
    probability = jnp.exp(scores - total_lse[..., None])
    prob_grad = jnp.einsum(
        "thd,pd->thp", scaled, prefix_keys[:, :value_width], preferred_element_type=jnp.float32
    )
    suffix_dot = jnp.sum(scaled.astype(jnp.float32) * suffix_out.astype(jnp.float32), axis=2)
    row_delta = (
        jnp.sum(probability * prob_grad, axis=2) + jnp.exp(tail_lse - total_lse) * suffix_dot
    )
    score_grad = (factor * probability * (prob_grad - row_delta[..., None])).astype(jnp.bfloat16)
    weights = probability.astype(jnp.bfloat16)
    query_grad = jnp.einsum(
        "thp,pd->thd", score_grad, prefix_keys, preferred_element_type=jnp.float32
    ).astype(jnp.bfloat16)

    def term_rows(first_row, row_count):
        key_term = jnp.einsum(
            "thp,thd->pd", score_grad, queries, preferred_element_type=jnp.float32
        )
        value_term = jnp.einsum("thp,thd->pd", weights, scaled, preferred_element_type=jnp.float32)
        return key_term + jnp.pad(value_term, ((0, 0), (0, key_term.shape[1] - value_width)))

    return (query_grad, term_rows)


def on_device(latent, queries, cotangent, suffix_out, suffix_lse, rewards, slot_sample):
    factor = softmax_scale()
    prefix_keys = lax.all_gather(latent, "prompt", axis=0, tiled=True)
    centred = rewards - jnp.mean(rewards)
    advantage_table = jnp.concatenate([centred, jnp.zeros((1,), jnp.float32)])
    sample_ids = jnp.arange(advantage_table.shape[0], dtype=jnp.int32)
    weight = jnp.sum(
        jnp.where(slot_sample[:, None] == sample_ids[None, :], advantage_table[None, :], 0.0),
        axis=1,
    )
    scaled = (weight[:, None, None] * cotangent.astype(jnp.float32)).astype(jnp.bfloat16)
    query_grad, term_rows = attend(queries, scaled, suffix_out, suffix_lse, prefix_keys, factor)
    prefix_count = prefix_keys.shape[0]
    owner_sums = lax.psum_scatter(
        term_rows(0, prefix_count), "prompt", scatter_dimension=0, tiled=True
    )
    latent_grad = lax.psum(owner_sums, "sample")
    return (query_grad, latent_grad)


def solution(mesh):
    in_specs = (
        P("prompt", None),
        P("prompt", "sample", None),
        P("prompt", "sample", None),
        P("prompt", "sample", None),
        P("prompt", "sample"),
        P(),
        P("prompt"),
    )
    out_specs = (P("prompt", "sample", None), P("prompt", None))
    return jax.shard_map(
        on_device, mesh=mesh, in_specs=in_specs, out_specs=out_specs, check_vma=False
    )
```

profile of v0, /device:TPU:0, one launch (start us, length us, event | category | flops | bytes accessed | tf_op | source)
XLA Modules:
  0.0 206.3 jit_solution(13262518655812535774)
XLA Ops:
  7.2 0.0 all-gather.2.cloned.1.call-start
  7.2 0.7 all-gather.2.cloned.1.call-update
  7.9 0.0 reduce-scatter.2.cloned.1.call-start
  7.9 1.3 reduce_sum.46
  9.9 0.7 broadcast_subtract_fusion
  10.5 0.1 pad_maximum_fusion
  10.6 0.8 select_reduce_fusion
  11.4 6.0 %multiply_reduce_fusion.2 = (f32[256,16]{1,0:T(8,128)S(1)}, bf16[256,16,512]{2,1,0:T(8,128)(2,1)}) fusion(bf16[256,16,512]{2,1,0:T(8,128)(2,1)} %param.10, bf16[256,16,512]{2,1,0:T(8,128)(2,1)} %param.9, f32[256]{0:T(256)S(1)} %select_reduce_fusion), kind=kLoop, calls=%fused_computation.7 | loop fusion | flops 14675968 | bytes 12600320 | tf_op jit(solution)/shard_map/reduce_sum | solution.py:29
  17.3 0.1 copy.25
  17.4 7.6 %copy.26 = bf16[256,16,512]{0,2,1:T(8,128)(2,1)} copy(bf16[256,16,512]{2,1,0:T(8,128)(2,1)} %get-tuple-element.3) | data formatting | bytes 8388608 | tf_op jit(solution)/shard_map/convert_element_type | solution.py:59
  25.0 4.9 %all-gather.2.cloned.1.call-done = bf16[1024,576]{0,1:T(8,128)(2,1)} async-done(((bf16[256,576]{0,1:T(8,128)(2,1)}), bf16[1024,576]{0,1:T(8,128)(2,1)}) %all-gather.2.cloned.1.call-update) | async-done | bytes 1179664 | tf_op jit(solution)/shard_map/all_gather | solution.py:51
  29.8 9.1 %multiply_reduce_fusion.1 = (f32[256,16]{0,1:T(8,128)S(1)}, f32[256,16,1024]{2,0,1:T(8,128)S(1)}) fusion(bf16[256,16,576]{0,2,1:T(8,128)(2,1)} %param.8, bf16[1024,576]{0,1:T(8,128)(2,1)} %all-gather.2.cloned.1.call-done), kind=kOutput, calls=%fused_computation.4 | convolution fusion | flops 4840222720 | bytes 22691840 | tf_op jit(solution)/shard_map/thd,pd->thp/dot_general | solution.py:17
  39.0 0.0 copy-start
  39.0 0.0 copy-start.4
  39.0 0.0 copy-start.1
  39.0 3.7 %exponential_reduce_fusion = f32[256,16]{0,1:T(8,128)S(1)} fusion(f32[256,16,1024]{2,0,1:T(8,128)S(1)} %get-tuple-element.5, f32[256,16]{0,1:T(8,128)S(1)} %get-tuple-element.4), kind=kLoop, calls=%fused_computation.3 | loop fusion | flops 12578816 | bytes 16809984 | tf_op jit(solution)/shard_map/reduce_sum | solution.py:21
  42.7 0.0 copy-done.4
  42.8 3.3 %copy-done = f32[256,16,1024]{2,0,1:T(8,128)} copy-done((f32[256,16,1024]{2,0,1:T(8,128)}, f32[256,16,1024]{2,0,1:T(8,128)S(1)}, u32[]{:S(2)}) %copy-start) | copy-done | bytes 16777240
  46.1 0.0 copy-done.1
  46.1 0.0 copy-start.3
  46.1 6.2 %fusion.5 = f32[1024,512]{0,1:T(8,128)} fusion(bf16[256,16,512]{0,2,1:T(8,128)(2,1)S(1)} %copy-done.1, f32[256,16,1024]{2,0,1:T(8,128)S(1)} %get-tuple-element.5, f32[256,16]{0,1:T(8,128)S(1)} %fusion.12), kind=kOutput, calls=%fused_computation.13 | convolution fusion | flops 4307550208 | bytes 23085056 | tf_op jit(solution)/shard_map/thp,thd->pd/dot_general | solution.py:43
  52.3 0.0 copy-done.3
  52.3 0.0 slice-start
  52.3 13.5 %multiply_reduce_fusion = (f32[256,16]{0,1:T(8,128)S(1)}, f32[256,16,1024]{2,0,1:T(8,128)}) fusion(f32[256,16,1024]{2,0,1:T(8,128)} %copy-done, f32[256,16]{0,1:T(8,128)S(1)} %fusion.12, bf16[256,16,512]{0,2,1:T(8,128)(2,1)S(1)} %copy-done.1, bf16[1024,576]{0,1:T(8,128)(2,1)S(1)} %copy-done.3), kind=kOutput, calls=%fused_computation.1 | convolution fusion | flops 4311740416 | bytes 38830080 | tf_op jit(solution)/shard_map/thd,pd->thp/dot_general | solution.py:26
  65.8 0.0 slice-start.1
  65.8 0.0 copy-start.5
  65.8 12.7 %multiply_convert_fusion = bf16[256,16,1024]{2,0,1:T(8,128)(2,1)S(1)} fusion(f32[256,16,1024]{2,0,1:T(8,128)} %get-tuple-element.7, f32[256,16,1024]{2,0,1:T(8,128)} %copy-done, f32[256,16]{0,1:T(8,128)S(1)} %fusion.20, f32[256,16]{0,1:T(8,128)S(1)} %fusion.12), kind=kLoop, calls=%fused_computation | loop fusion | flops 25165824 | bytes 41975808 | tf_op jit(solution)/shard_map/convert_element_type | solution.py:33
  78.6 0.0 copy-start.2
  78.6 3.2 %copy-done.2 = bf16[256,16,1024]{2,0,1:T(8,128)(2,1)} copy-done((bf16[256,16,1024]{2,0,1:T(8,128)(2,1)}, bf16[256,16,1024]{2,0,1:T(8,128)(2,1)S(1)}, u32[]{:S(2)}) %copy-start.2) | copy-done | bytes 8388632
  81.8 0.0 slice-done
  81.8 0.0 slice-done.1
  81.8 0.0 copy-done.5
  81.8 6.5 %bitcast_add_fusion = f32[1024,576]{0,1:T(8,128)} fusion(f32[1024,512]{0,1:T(8,128)S(1)} %copy-done.5, bf16[256,16,576]{0,2,1:T(8,128)(2,1)S(1)} %bitcast.23, bf16[256,16,1024]{2,0,1:T(8,128)(2,1)S(1)} %multiply_convert_fusion), kind=kOutput, calls=%fused_computation.12 | convolution fusion | flops 4832428032 | bytes 17563648 | tf_op jit(solution)/shard_map/thp,thd->pd/dot_general | solution.py:40
  88.3 0.0 reduce-scatter.2.cloned.1.call-update
  88.3 0.0 all-reduce.3.cloned.1.call-start
  88.4 32.9 %reduce-scatter.2.cloned.1.call-done = f32[256,576]{0,1:T(8,128)} async-done(((f32[1024,576]{0,1:T(8,128)}), f32[256,576]{0,1:T(8,128)}) %reduce-scatter.2.cloned.1.call-update) | async-done | bytes 589840 | tf_op jit(solution)/shard_map/reduce_scatter | solution.py:62
  121.3 0.0 all-reduce.3.cloned.1.call-update
  121.3 10.1 %convolution_convert_fusion = bf16[256,16,576]{0,2,1:T(8,128)(2,1)} fusion(bf16[256,16,1024]{2,0,1:T(8,128)(2,1)} %copy-done.2, bf16[1024,576]{0,1:T(8,128)(2,1)S(1)} %copy-done.3), kind=kOutput, calls=%fused_computation.11 | convolution fusion | flops 4834197504 | bytes 14286848 | tf_op jit(solution)/shard_map/thp,pd->thd/dot_general | solution.py:35
  131.4 66.5 %all-reduce.3.cloned.1.call-done = f32[256,576]{0,1:T(8,128)} async-done(((f32[256,576]{0,1:T(8,128)}), f32[256,576]{0,1:T(8,128)}) %all-reduce.3.cloned.1.call-update) | async-done | bytes 589840 | tf_op jit(solution)/shard_map/psum | solution.py:65
  197.9 1.9 copy.30
  (3 shorter events, 0.0 us)
Async XLA Ops:
  7.2 22.7 %all-gather.2.cloned.1.call-start = ((), (), s32[]{:S(2)}) async-start(), calls=%async_computation.1 | async-start | bytes 1474560 | tf_op jit(solution)/shard_map/all_gather | solution.py:51
  7.9 113.4 %reduce-scatter.2.cloned.1.call-start = ((), (), s32[]{:S(2)}) async-start(), calls=%async_computation.2 | async-start | bytes 2949120 | tf_op jit(solution)/shard_map/reduce_scatter | solution.py:62
  39.0 7.1 %copy-start = (f32[256,16,1024]{2,0,1:T(8,128)}, f32[256,16,1024]{2,0,1:T(8,128)S(1)}, u32[]{:S(2)}) copy-start(f32[256,16,1024]{2,0,1:T(8,128)S(1)} %get-tuple-element.5) | copy-start | bytes 50331652
  39.0 3.7 %copy-start.4 = (bf16[256,16]{0,1:T(8,128)(2,1)S(1)}, bf16[256,16]{0,1:T(8,128)(2,1)}, u32[]{:S(2)}) copy-start(bf16[256,16]{0,1:T(8,128)(2,1)} %param.11) | copy-start | bytes 24580
  39.0 7.1 %copy-start.1 = (bf16[256,16,512]{0,2,1:T(8,128)(2,1)S(1)}, bf16[256,16,512]{0,2,1:T(8,128)(2,1)}, u32[]{:S(2)}) copy-start(bf16[256,16,512]{0,2,1:T(8,128)(2,1)} %copy.26) | copy-start | bytes 12582916
  46.1 6.2 %copy-start.3 = (bf16[1024,576]{0,1:T(8,128)(2,1)S(1)}, bf16[1024,576]{0,1:T(8,128)(2,1)}, u32[]{:S(2)}) copy-start(bf16[1024,576]{0,1:T(8,128)(2,1)} %all-gather.2.cloned.1.call-done) | copy-start | bytes 3538948
  52.3 29.5 %slice-start = ((s8[4718592]{0:T(1024)(128)(4,1)}), s8[524288]{0:T(1024)(128)(4,1)S(1)}, s32[]{:S(2)}) async-start(s8[4718592]{0:T(1024)(128)(4,1)} %bitcast.22), calls=%async_computation.4 | async-start | bytes 1048576
  65.8 16.0 %slice-start.1 = ((s8[4718592]{0:T(1024)(128)(4,1)}), s8[4194304]{0:T(1024)(128)(4,1)S(1)}, s32[]{:S(2)}) async-start(s8[4718592]{0:T(1024)(128)(4,1)} %bitcast.22), calls=%async_computation.5 | async-start | bytes 8388608
  65.8 16.0 %copy-start.5 = (f32[1024,512]{0,1:T(8,128)S(1)}, f32[1024,512]{0,1:T(8,128)}, u32[]{:S(2)}) copy-start(f32[1024,512]{0,1:T(8,128)} %fusion.5) | copy-start | bytes 6291460
  78.6 3.2 %copy-start.2 = (bf16[256,16,1024]{2,0,1:T(8,128)(2,1)}, bf16[256,16,1024]{2,0,1:T(8,128)(2,1)S(1)}, u32[]{:S(2)}) copy-start(bf16[256,16,1024]{2,0,1:T(8,128)(2,1)S(1)} %multiply_convert_fusion) | copy-start | bytes 25165828
  88.3 109.6 %all-reduce.3.cloned.1.call-start = ((), (), s32[]{:S(2)}) async-start(), calls=%async_computation.3 | async-start | bytes 1179648 | tf_op jit(solution)/shard_map/psum | solution.py:65
Sparse Core Ops, SparseCore 0:
  9.5 20.2 all-gather.1
  88.4 32.7 reduce-scatter.1
  124.6 73.2 all-reduce.2
where the time goes:
time: 207 us; the launch traced here: 206 us
  waiting for transfers between devices  105 us (51%)
  matrix products  45.4 us (22%)
  other arithmetic  25.2 us (12%)
  local copies, waits for them, and re-layouts  16.1 us (8%)
  between operations  14.5 us (7%)
    psum x1, waiting for transfers between devices, on_device(): latent_grad = lax.psum(owner_sums, 'sample')  66.5 us
    reduce_scatter x1, waiting for transfers between devices, on_device(): lax.psum_scatter(term_rows(0, prefix_count), 'prompt', scatter_dimension=...  32.9 us
    dot_general x1, matrix products, attend(): jnp.einsum('thd,pd->thp', scaled, prefix_keys[:, :value_width], preferred...  13.5 us
    convert_element_type x1, other arithmetic, attend(): (factor * probability * (prob_grad - row_delta[..., None])).astype(jnp.bf...  12.7 us
    dot_general x1, matrix products, attend(): jnp.einsum('thp,pd->thd', score_grad, prefix_keys, preferred_element_type...  10.1 us
    dot_general x1, matrix products, attend(): jnp.einsum('thd,pd->thp', queries, prefix_keys, preferred_element_type=jn...  9.15 us
    unnamed x17, local copies, waits for them, and re-layouts  8.49 us
    convert_element_type x1, local copies, waits for them, and re-layouts, on_device(): (weight[:, None, None] * cotangent.astype(jnp.float32)).astype(jnp.bfloat16)  7.59 us
  transfers between devices with their start and end apart: 3, of which 3 were waited for; matrix products, arithmetic and copies ran while one was open for 13% of the time, Pallas kernels for 0%

commit v1 on v0

--- a/solution.py
+++ b/solution.py
@@ -62,7 +62,11 @@
     owner_sums = lax.psum_scatter(
         term_rows(0, prefix_count), "prompt", scatter_dimension=0, tiled=True
     )
-    latent_grad = lax.psum(owner_sums, "sample")
+    latent_grad = owner_sums
+    for hop in (1, 2, 4):
+        latent_grad = latent_grad + lax.ppermute(
+            latent_grad, "sample", [(dev, dev ^ hop) for dev in range(8)]
+        )
     return (query_grad, latent_grad)
 
 

time: 207 us -> 187 us (0.903)
  waiting for transfers between devices: 105 us -> 79 us
  starting transfers between devices: 0.12 us -> 5.54 us
  other arithmetic: 25.2 us -> 27.3 us
    psum x1 -> x0, waiting for transfers between devices: 66.5 us -> none  [on_device(): latent_grad = lax.psum(owner_sums, 'sample')]
    ppermute x0 -> x3, waiting for transfers between devices: none -> 40.5 us  [on_device(): lax.ppermute(latent_grad, 'sample', [(dev, dev ^ hop) for dev in range(8)])]
    ppermute x0 -> x3, starting transfers between devices: none -> 5.46 us  [on_device(): lax.ppermute(latent_grad, 'sample', [(dev, dev ^ hop) for dev in range(8)])]
    add x0 -> x3, other arithmetic: none -> 2.11 us  [on_device(): latent_grad + lax.ppermute(latent_grad, 'sample', [(dev, dev ^ hop) for d...]
    unnamed x17 -> x16, local copies, waits for them, and re-layouts: 8.49 us -> 6.56 us
  transfers between devices with their start and end apart: 3 -> 5, of which waited for: 3 -> 5; matrix products, arithmetic and copies ran while one was open for 13% -> 14% of each run, Pallas kernels for 0% -> 0%
where the time goes in v1:
time: 187 us; the launch traced here: 186 us
  waiting for transfers between devices  79 us (42%)
  matrix products  45.4 us (24%)
  other arithmetic  27.3 us (15%)
  between operations  14.8 us (8%)
  local copies, waits for them, and re-layouts  14.2 us (8%)
  starting transfers between devices  5.54 us (3%)
    ppermute x3, waiting for transfers between devices, on_device(): lax.ppermute(latent_grad, 'sample', [(dev, dev ^ hop) for dev in range(8)])  40.5 us
    reduce_scatter x1, waiting for transfers between devices, on_device(): lax.psum_scatter(term_rows(0, prefix_count), 'prompt', scatter_dimension=...  32.9 us
    dot_general x1, matrix products, attend(): jnp.einsum('thd,pd->thp', scaled, prefix_keys[:, :value_width], preferred...  13.5 us
    convert_element_type x1, other arithmetic, attend(): (factor * probability * (prob_grad - row_delta[..., None])).astype(jnp.bf...  12.7 us
    dot_general x1, matrix products, attend(): jnp.einsum('thp,pd->thd', score_grad, prefix_keys, preferred_element_type...  10.1 us
    dot_general x1, matrix products, attend(): jnp.einsum('thd,pd->thp', queries, prefix_keys, preferred_element_type=jn...  9.15 us
    convert_element_type x1, local copies, waits for them, and re-layouts, on_device(): (weight[:, None, None] * cotangent.astype(jnp.float32)).astype(jnp.bfloat16)  7.56 us
    unnamed x16, local copies, waits for them, and re-layouts  6.56 us
  transfers between devices with their start and end apart: 5, of which 5 were waited for; matrix products, arithmetic and copies ran while one was open for 14% of the time, Pallas kernels for 0%

profile of v1, /device:TPU:0, one launch (start us, length us, event | category | flops | bytes accessed | tf_op | source)
XLA Modules:
  0.0 186.2 jit_solution(14437693251459643378)
XLA Ops:
  7.2 0.0 all-gather.2.cloned.1.call-start
  7.2 0.7 all-gather.2.cloned.1.call-update
  7.9 0.0 reduce-scatter.2.cloned.1.call-start
  7.9 1.3 reduce_sum.46
  9.9 0.7 broadcast_subtract_fusion
  10.5 0.1 pad_maximum_fusion
  10.6 0.8 select_reduce_fusion
  11.4 6.0 %multiply_reduce_fusion.2 = (f32[256,16]{1,0:T(8,128)S(1)}, bf16[256,16,512]{2,1,0:T(8,128)(2,1)}) fusion(bf16[256,16,512]{2,1,0:T(8,128)(2,1)} %param.10, bf16[256,16,512]{2,1,0:T(8,128)(2,1)} %param.9, f32[256]{0:T(256)S(1)} %select_reduce_fusion), kind=kLoop, calls=%fused_computation.7 | loop fusion | flops 14675968 | bytes 12600320 | tf_op jit(solution)/shard_map/reduce_sum | solution.py:29
  17.3 0.1 copy.25
  17.4 7.6 %copy.26 = bf16[256,16,512]{0,2,1:T(8,128)(2,1)} copy(bf16[256,16,512]{2,1,0:T(8,128)(2,1)} %get-tuple-element.3) | data formatting | bytes 8388608 | tf_op jit(solution)/shard_map/convert_element_type | solution.py:59
  24.9 4.9 %all-gather.2.cloned.1.call-done = bf16[1024,576]{0,1:T(8,128)(2,1)} async-done(((bf16[256,576]{0,1:T(8,128)(2,1)}), bf16[1024,576]{0,1:T(8,128)(2,1)}) %all-gather.2.cloned.1.call-update) | async-done | bytes 1179664 | tf_op jit(solution)/shard_map/all_gather | solution.py:51
  29.8 9.1 %multiply_reduce_fusion.1 = (f32[256,16]{0,1:T(8,128)S(1)}, f32[256,16,1024]{2,0,1:T(8,128)S(1)}) fusion(bf16[256,16,576]{0,2,1:T(8,128)(2,1)} %param.8, bf16[1024,576]{0,1:T(8,128)(2,1)} %all-gather.2.cloned.1.call-done), kind=kOutput, calls=%fused_computation.4 | convolution fusion | flops 4840222720 | bytes 22691840 | tf_op jit(solution)/shard_map/thd,pd->thp/dot_general | solution.py:17
  39.0 0.0 copy-start
  39.0 0.0 copy-start.4
  39.0 0.0 copy-start.1
  39.0 3.7 %exponential_reduce_fusion = f32[256,16]{0,1:T(8,128)S(1)} fusion(f32[256,16,1024]{2,0,1:T(8,128)S(1)} %get-tuple-element.5, f32[256,16]{0,1:T(8,128)S(1)} %get-tuple-element.4), kind=kLoop, calls=%fused_computation.3 | loop fusion | flops 12578816 | bytes 16809984 | tf_op jit(solution)/shard_map/reduce_sum | solution.py:21
  42.7 0.0 copy-done.4
  42.8 3.3 %copy-done = f32[256,16,1024]{2,0,1:T(8,128)} copy-done((f32[256,16,1024]{2,0,1:T(8,128)}, f32[256,16,1024]{2,0,1:T(8,128)S(1)}, u32[]{:S(2)}) %copy-start) | copy-done | bytes 16777240
  46.1 0.0 copy-done.1
  46.1 0.0 copy-start.3
  46.1 6.2 %fusion.5 = f32[1024,512]{0,1:T(8,128)} fusion(bf16[256,16,512]{0,2,1:T(8,128)(2,1)S(1)} %copy-done.1, f32[256,16,1024]{2,0,1:T(8,128)S(1)} %get-tuple-element.5, f32[256,16]{0,1:T(8,128)S(1)} %fusion.12), kind=kOutput, calls=%fused_computation.13 | convolution fusion | flops 4307550208 | bytes 23085056 | tf_op jit(solution)/shard_map/thp,thd->pd/dot_general | solution.py:43
  52.3 0.0 copy-done.3
  52.3 0.0 slice-start
  52.3 13.5 %multiply_reduce_fusion = (f32[256,16]{0,1:T(8,128)S(1)}, f32[256,16,1024]{2,0,1:T(8,128)}) fusion(f32[256,16,1024]{2,0,1:T(8,128)} %copy-done, f32[256,16]{0,1:T(8,128)S(1)} %fusion.12, bf16[256,16,512]{0,2,1:T(8,128)(2,1)S(1)} %copy-done.1, bf16[1024,576]{0,1:T(8,128)(2,1)S(1)} %copy-done.3), kind=kOutput, calls=%fused_computation.1 | convolution fusion | flops 4311740416 | bytes 38830080 | tf_op jit(solution)/shard_map/thd,pd->thp/dot_general | solution.py:26
  65.8 0.0 slice-start.1
  65.8 0.0 copy-start.5
  65.8 12.7 %multiply_convert_fusion = bf16[256,16,1024]{2,0,1:T(8,128)(2,1)S(1)} fusion(f32[256,16,1024]{2,0,1:T(8,128)} %get-tuple-element.7, f32[256,16,1024]{2,0,1:T(8,128)} %copy-done, f32[256,16]{0,1:T(8,128)S(1)} %fusion.20, f32[256,16]{0,1:T(8,128)S(1)} %fusion.12), kind=kLoop, calls=%fused_computation | loop fusion | flops 25165824 | bytes 41975808 | tf_op jit(solution)/shard_map/convert_element_type | solution.py:33
  78.5 0.0 copy-start.2
  78.5 3.2 %copy-done.2 = bf16[256,16,1024]{2,0,1:T(8,128)(2,1)} copy-done((bf16[256,16,1024]{2,0,1:T(8,128)(2,1)}, bf16[256,16,1024]{2,0,1:T(8,128)(2,1)S(1)}, u32[]{:S(2)}) %copy-start.2) | copy-done | bytes 8388632
  81.7 0.0 slice-done
  81.8 0.0 slice-done.1
  81.8 0.0 copy-done.5
  81.8 6.5 %bitcast_add_fusion = f32[1024,576]{0,1:T(8,128)} fusion(f32[1024,512]{0,1:T(8,128)S(1)} %copy-done.5, bf16[256,16,576]{0,2,1:T(8,128)(2,1)S(1)} %bitcast.23, bf16[256,16,1024]{2,0,1:T(8,128)(2,1)S(1)} %multiply_convert_fusion), kind=kOutput, calls=%fused_computation.12 | convolution fusion | flops 4832428032 | bytes 17563648 | tf_op jit(solution)/shard_map/thp,thd->pd/dot_general | solution.py:40
  88.3 0.0 reduce-scatter.2.cloned.1.call-update
  88.3 32.9 %reduce-scatter.2.cloned.1.call-done = f32[256,576]{0,1:T(8,128)} async-done(((f32[1024,576]{0,1:T(8,128)}), f32[256,576]{0,1:T(8,128)}) %reduce-scatter.2.cloned.1.call-update) | async-done | bytes 589840 | tf_op jit(solution)/shard_map/reduce_scatter | solution.py:62
  121.2 1.5 collective-permute-start
  122.7 13.6 %collective-permute-done = f32[256,576]{0,1:T(8,128)S(1)} collective-permute-done((f32[256,576]{0,1:T(8,128)}, f32[256,576]{0,1:T(8,128)S(1)}, u32[]{:S(2)}, u32[]{:S(2)}) %collective-permute-start) | collective-permute-done | bytes 589856 | tf_op jit(solution)/shard_map/ppermute | solution.py:67
  136.3 1.1 add.33
  137.5 1.6 collective-permute-start.1
  139.0 12.6 %collective-permute-done.1 = f32[256,576]{0,1:T(8,128)S(1)} collective-permute-done((f32[256,576]{0,1:T(8,128)S(1)}, f32[256,576]{0,1:T(8,128)S(1)}, u32[]{:S(2)}, u32[]{:S(2)}) %collective-permute-start.1) | collective-permute-done | bytes 589856 | tf_op jit(solution)/shard_map/ppermute | solution.py:67
  151.6 0.1 add.34
  151.7 2.4 %collective-permute-start.2 = (f32[256,576]{0,1:T(8,128)S(1)}, f32[256,576]{0,1:T(8,128)S(1)}, u32[]{:S(2)}, u32[]{:S(2)}) collective-permute-start(f32[256,576]{0,1:T(8,128)S(1)} %add.34), channel_id=1, source_target_pairs={{0,4},{1,5},{2,6},{3,7},{4,0},{5,1},{6,2},{7,3},{8,12},{9,13},{10,... | collective-permute-start | bytes 1769480 | tf_op jit(solution)/shard_map/ppermute | solution.py:67
  154.1 10.1 %convolution_convert_fusion = bf16[256,16,576]{0,2,1:T(8,128)(2,1)} fusion(bf16[256,16,1024]{2,0,1:T(8,128)(2,1)} %copy-done.2, bf16[1024,576]{0,1:T(8,128)(2,1)S(1)} %copy-done.3), kind=kOutput, calls=%fused_computation.11 | convolution fusion | flops 4834197504 | bytes 14286848 | tf_op jit(solution)/shard_map/thp,pd->thd/dot_general | solution.py:35
  164.2 14.3 %collective-permute-done.2 = f32[256,576]{0,1:T(8,128)S(1)} collective-permute-done((f32[256,576]{0,1:T(8,128)S(1)}, f32[256,576]{0,1:T(8,128)S(1)}, u32[]{:S(2)}, u32[]{:S(2)}) %collective-permute-start.2) | collective-permute-done | bytes 589856 | tf_op jit(solution)/shard_map/ppermute | solution.py:67
  178.5 0.9 add.35
  (3 shorter events, 0.0 us)
Async XLA Ops:
  7.2 22.7 %all-gather.2.cloned.1.call-start = ((), (), s32[]{:S(2)}) async-start(), calls=%async_computation.1 | async-start | bytes 1474560 | tf_op jit(solution)/shard_map/all_gather | solution.py:51
  7.9 113.3 %reduce-scatter.2.cloned.1.call-start = ((), (), s32[]{:S(2)}) async-start(), calls=%async_computation.2 | async-start | bytes 2949120 | tf_op jit(solution)/shard_map/reduce_scatter | solution.py:62
  39.0 7.1 %copy-start = (f32[256,16,1024]{2,0,1:T(8,128)}, f32[256,16,1024]{2,0,1:T(8,128)S(1)}, u32[]{:S(2)}) copy-start(f32[256,16,1024]{2,0,1:T(8,128)S(1)} %get-tuple-element.5) | copy-start | bytes 50331652
  39.0 3.7 %copy-start.4 = (bf16[256,16]{0,1:T(8,128)(2,1)S(1)}, bf16[256,16]{0,1:T(8,128)(2,1)}, u32[]{:S(2)}) copy-start(bf16[256,16]{0,1:T(8,128)(2,1)} %param.11) | copy-start | bytes 24580
  39.0 7.1 %copy-start.1 = (bf16[256,16,512]{0,2,1:T(8,128)(2,1)S(1)}, bf16[256,16,512]{0,2,1:T(8,128)(2,1)}, u32[]{:S(2)}) copy-start(bf16[256,16,512]{0,2,1:T(8,128)(2,1)} %copy.26) | copy-start | bytes 12582916
  46.1 6.2 %copy-start.3 = (bf16[1024,576]{0,1:T(8,128)(2,1)S(1)}, bf16[1024,576]{0,1:T(8,128)(2,1)}, u32[]{:S(2)}) copy-start(bf16[1024,576]{0,1:T(8,128)(2,1)} %all-gather.2.cloned.1.call-done) | copy-start | bytes 3538948
  52.3 29.5 %slice-start = ((s8[4718592]{0:T(1024)(128)(4,1)}), s8[524288]{0:T(1024)(128)(4,1)S(1)}, s32[]{:S(2)}) async-start(s8[4718592]{0:T(1024)(128)(4,1)} %bitcast.22), calls=%async_computation.3 | async-start | bytes 1048576
  65.8 16.0 %slice-start.1 = ((s8[4718592]{0:T(1024)(128)(4,1)}), s8[4194304]{0:T(1024)(128)(4,1)S(1)}, s32[]{:S(2)}) async-start(s8[4718592]{0:T(1024)(128)(4,1)} %bitcast.22), calls=%async_computation.4 | async-start | bytes 8388608
  65.8 16.0 %copy-start.5 = (f32[1024,512]{0,1:T(8,128)S(1)}, f32[1024,512]{0,1:T(8,128)}, u32[]{:S(2)}) copy-start(f32[1024,512]{0,1:T(8,128)} %fusion.5) | copy-start | bytes 6291460
  78.5 3.2 %copy-start.2 = (bf16[256,16,1024]{2,0,1:T(8,128)(2,1)}, bf16[256,16,1024]{2,0,1:T(8,128)(2,1)S(1)}, u32[]{:S(2)}) copy-start(bf16[256,16,1024]{2,0,1:T(8,128)(2,1)S(1)} %multiply_convert_fusion) | copy-start | bytes 25165828
  121.2 15.1 %collective-permute-start = (f32[256,576]{0,1:T(8,128)}, f32[256,576]{0,1:T(8,128)S(1)}, u32[]{:S(2)}, u32[]{:S(2)}) collective-permute-start(f32[256,576]{0,1:T(8,128)} %reduce-scatter.2.cloned.1.call-done), channel_id=1, source_target_pairs={{0,1},{1,0},{2,3},{3,2},{4,5},{5,4},{6,7},{7,6},{8,9},{9,8},{10,11... | collective-permute-start | bytes 1769480 | tf_op jit(solution)/shard_map/ppermute | solution.py:67
  137.5 14.1 %collective-permute-start.1 = (f32[256,576]{0,1:T(8,128)S(1)}, f32[256,576]{0,1:T(8,128)S(1)}, u32[]{:S(2)}, u32[]{:S(2)}) collective-permute-start(f32[256,576]{0,1:T(8,128)S(1)} %add.33), channel_id=1, source_target_pairs={{0,2},{1,3},{2,0},{3,1},{4,6},{5,7},{6,4},{7,5},{8,10},{9,11},{10,... | collective-permute-start | bytes 1769480 | tf_op jit(solution)/shard_map/ppermute | solution.py:67
  151.7 26.8 %collective-permute-start.2 = (f32[256,576]{0,1:T(8,128)S(1)}, f32[256,576]{0,1:T(8,128)S(1)}, u32[]{:S(2)}, u32[]{:S(2)}) collective-permute-start(f32[256,576]{0,1:T(8,128)S(1)} %add.34), channel_id=1, source_target_pairs={{0,4},{1,5},{2,6},{3,7},{4,0},{5,1},{6,2},{7,3},{8,12},{9,13},{10,... | collective-permute-start | bytes 1769480 | tf_op jit(solution)/shard_map/ppermute | solution.py:67
Sparse Core Ops, SparseCore 0:
  9.5 20.2 all-gather.1
  88.4 32.7 reduce-scatter.1
